TPU v7x, 32 devices: a whole 2x2x4 slice. The times are simulated.
32 devices in a mesh: groups: 2 (over x), tr: 16 (over z, y, core).
Axes of the slice: x: 2, y: 2, z: 4, core: 2. Of those that a mesh axis runs over, the one named last changes fastest.
Arguments:
- object_field: float32 [2, 16384, 1024], P(None, ('groups', 'tr')), parts along dimension 1, may hold values from -6 to 6
- probe_modes: float32 [2, 2, 256, 256], replicated, may hold values from -96 to 96
- scan_offsets: int32 [32, 8, 2], P(('groups', 'tr')), parts along dimension 0, may hold values from 0 to 768, as said below
- scan_counts: int32 [32], P(('groups', 'tr')), parts along dimension 0, may hold values from 1 to 8, as said below
- measured: int32 [32, 8, 256, 256], P(('groups', 'tr')), parts along dimension 0, may hold values from 0 to 4096
Outputs:
- object_grad: float32 [2, 16384, 1024], P(None, ('groups', 'tr')), parts along dimension 1
- probe_grad: float32 [2048, 256], P(('groups', 'tr')), parts along dimension 0
There are 2 independent parts, one for each index of `groups`. A program takes and returns all parts, laid end to end along the dimension named above; an argument that names none is the same for every part. Nothing has to cross between parts.
Inputs may be any that keep to these rules, and one draw needn't show every extreme that they name: `scan_counts`: each tile has 1 to 8 used scan positions, and some tile has exactly 8. `scan_offsets`: row offsets lie in 0 to 511 within the tile, column offsets in 0 to 768; both ends are reached; every slot holds a valid offset, used or not.
All inputs are finite; a program needn't handle non-finite values.
Results may differ from a plain program's by a relative error of at most 0.0095.
Values may be sent and summed in bfloat16 or wider, within the bound.
No kernel may reach another device: no remote copies, remote signals or barrier semaphores. Data moves between devices by JAX's collectives and lax.ppermute only.
A program may use at most 64 MiB of HBM per device.

v0:
```python
import jax
import jax.numpy as jnp
from jax import lax
from jax.sharding import PartitionSpec as P

loss_scale = 1.0 / 1024.0


def shifted(value, axis, steps):
    count = lax.axis_size(axis)
    initial, last = (max(0, -steps), min(count, count - steps))
    return lax.ppermute(value, axis, [(source, source + steps) for source in range(initial, last)])


def dft_table(patch_size):
    index_run = jnp.arange(patch_size, dtype=jnp.int32)
    product = index_run[:, None] * index_run[None, :] % patch_size
    phase_angle = -2.0 * jnp.pi / patch_size * product.astype(jnp.float32)
    unit_scale = 1.0 / jnp.sqrt(jnp.float32(patch_size))
    table_real = jnp.cos(phase_angle) * unit_scale
    table_imag = jnp.sin(phase_angle) * unit_scale
    upper_rows = jnp.concatenate([table_real, table_imag], axis=1)
    lower_rows = jnp.concatenate([-table_imag, table_real], axis=1)
    return jnp.concatenate([upper_rows, lower_rows], axis=0).astype(jnp.bfloat16)


def forward_part(patch, sqrt_counts, probe_modes, dft_matrix):
    patch_size = patch.shape[-1]
    mode_count = probe_modes.shape[0]
    probe_real = probe_modes[:, 0]
    probe_imag = probe_modes[:, 1]
    object_real = patch[0]
    object_imag = patch[1]
    exit_real = probe_real * object_real - probe_imag * object_imag
    exit_imag = probe_real * object_imag + probe_imag * object_real
    exit_wave = jnp.concatenate([exit_real, exit_imag], axis=-1).astype(jnp.bfloat16)
    half_done = jnp.einsum(
        "mpk,kl->mpl", exit_wave, dft_matrix, preferred_element_type=jnp.float32
    ).astype(jnp.bfloat16)
    stacked = jnp.concatenate([half_done[..., :patch_size], half_done[..., patch_size:]], axis=1)
    far_field = jnp.einsum("kq,mkp->mqp", dft_matrix, stacked, preferred_element_type=jnp.float32)
    far_real = far_field[:, :patch_size]
    far_imag = far_field[:, patch_size:]
    model_power = jnp.sum(far_real * far_real + far_imag * far_imag, axis=0)
    factor = 2.0 * loss_scale * (1.0 - sqrt_counts / jnp.sqrt(model_power + 1.0))
    return (
        (far_field.reshape(mode_count, 2, patch_size, patch_size) * factor)
        .reshape(mode_count, 2 * patch_size, patch_size)
        .astype(jnp.bfloat16)
    )


def backward_part(grad_far, patch, probe_modes, dft_matrix):
    patch_size = patch.shape[-1]
    probe_real = probe_modes[:, 0]
    probe_imag = probe_modes[:, 1]
    object_real = patch[0]
    object_imag = patch[1]
    back_rows = jnp.einsum(
        "qk,mkp->mqp", dft_matrix, grad_far, preferred_element_type=jnp.float32
    ).astype(jnp.bfloat16)
    col_major = jnp.concatenate([back_rows[:, :patch_size], back_rows[:, patch_size:]], axis=-1)
    grad_wave = jnp.einsum("mpk,lk->mpl", col_major, dft_matrix, preferred_element_type=jnp.float32)
    grad_real = grad_wave[..., :patch_size]
    grad_imag = grad_wave[..., patch_size:]
    obj_real = jnp.sum(probe_real * grad_real + probe_imag * grad_imag, axis=0)
    obj_imag = jnp.sum(probe_real * grad_imag - probe_imag * grad_real, axis=0)
    probe_greal = object_real * grad_real + object_imag * grad_imag
    probe_gimag = object_real * grad_imag - object_imag * grad_real
    return (jnp.stack([obj_real, obj_imag]), jnp.stack([probe_greal, probe_gimag], axis=1))


def patch_grads(patch, sqrt_counts, probe_modes, dft_matrix):
    grad_far = forward_part(patch, sqrt_counts, probe_modes, dft_matrix)
    return backward_part(grad_far, patch, probe_modes, dft_matrix)


def add_block(gradient, block, offset_pair):
    corner = (jnp.int32(0), offset_pair[0], offset_pair[1])
    current = lax.dynamic_slice(gradient, corner, block.shape)
    return lax.dynamic_update_slice(gradient, current + block, corner)


def on_device(object_field, probe_modes, scan_offsets, scan_counts, measured):
    patch_size = probe_modes.shape[-1]
    strip_rows = object_field.shape[1]
    dft_matrix = dft_table(patch_size)
    lower_band = shifted(object_field[:, :patch_size, :], "tr", -1)
    extended = jnp.concatenate([object_field, lower_band], axis=1)
    sqrt_counts = jnp.sqrt(measured[0].astype(jnp.float32))
    offsets = scan_offsets[0]
    own_count = scan_counts[0]

    def extract_patch(offset_pair):
        return lax.dynamic_slice(
            extended, (jnp.int32(0), offset_pair[0], offset_pair[1]), (2, patch_size, patch_size)
        )

    def local_slot(slot_index, loop_state):
        gradient, probe_sum = loop_state
        offset_pair = offsets[slot_index]
        part_object, part_probe = patch_grads(
            extract_patch(offset_pair), sqrt_counts[slot_index], probe_modes, dft_matrix
        )
        return (add_block(gradient, part_object, offset_pair), probe_sum + part_probe)

    zero_grad = jnp.zeros(extended.shape, jnp.float32)
    zero_probe = jnp.zeros(probe_modes.shape, jnp.float32)
    gradient, probe_sum = lax.fori_loop(
        jnp.int32(0), own_count, local_slot, (zero_grad, zero_probe)
    )
    edge_grad = shifted(gradient[:, strip_rows:, :], "tr", 1)
    object_grad = gradient[:, :strip_rows, :] + jnp.pad(
        edge_grad, ((0, 0), (0, strip_rows - patch_size), (0, 0))
    )
    flat_probe = probe_sum.reshape(-1, patch_size)
    whole_probe = lax.psum(flat_probe, "tr")
    share_rows = flat_probe.shape[0] // lax.axis_size("tr")
    probe_grad = lax.dynamic_slice_in_dim(
        whole_probe, lax.axis_index("tr") * share_rows, share_rows, 0
    )
    return (object_grad, probe_grad)


def solution(mesh):
    return jax.shard_map(
        on_device,
        mesh=mesh,
        in_specs=(
            P(None, ("groups", "tr"), None),
            P(),
            P(("groups", "tr"), None, None),
            P(("groups", "tr")),
            P(("groups", "tr"), None, None, None),
        ),
        out_specs=(P(None, ("groups", "tr"), None), P(("groups", "tr"), None)),
        check_vma=False,
    )
```

profile of v0, /device:TPU:0, one launch (start us, length us, event | category | flops | bytes accessed | tf_op | source)
XLA Modules:
  0.0 312.3 jit_solution(7520786833410476199)
XLA Ops:
  7.2 0.0 copy-start.1
  7.2 0.0 all-reduce.3.cloned.1.call-start
  7.2 3.2 %slice.59 = f32[2,256,1024]{2,1,0:T(8,128)} slice(f32[2,512,1024]{2,1,0:T(8,128)} %param.7), slice={[0:2], [0:256], [0:1024]} | slice | bytes 4194304 | tf_op jit(solution)/shard_map/slice | solution.py:88
  10.5 1.3 collective-permute-start
  11.7 0.0 copy-done.1
  11.8 0.1 copy.10
  11.8 2.9 copy.9
  14.8 0.0 copy-start
  14.8 1.0 fusion.37
  15.8 1.1 negate_convert_fusion
  16.9 3.5 %sqrt_bitcast_fusion = f32[8,256,256]{1,2,0:T(8,128)} fusion(s32[1,8,256,256]{2,3,1,0:T(8,128)} %copy.9), kind=kLoop, calls=%fused_computation.55 | loop fusion | flops 524288 | bytes 4194304 | tf_op jit(solution)/shard_map/sqrt | solution.py:90
  20.4 0.0 collective-permute-done
  20.4 0.0 copy-done
  20.4 5.1 %pad_maximum_fusion = f32[2,768,1024]{2,1,0:T(8,128)} fusion(f32[2,256,1024]{2,1,0:T(8,128)} %collective-permute-done, f32[2,512,1024]{2,1,0:T(8,128)S(1)} %copy-done), kind=kLoop, calls=%fused_computation.53 | loop fusion | flops 1572864 | bytes 12582912 | tf_op jit(solution)/shard_map/concatenate | solution.py:89
  25.5 0.0 copy-start.2
  25.5 0.1 broadcast_in_dim.10
  25.6 3.4 %broadcast_in_dim.4 = f32[2,768,1024]{2,1,0:T(8,128)} broadcast(f32[]{:T(128)} %constant.22.clone.1), dimensions={} | broadcast | bytes 6291460 | tf_op jit(solution)/shard_map/broadcast_in_dim | solution.py:107
  29.0 0.0 copy-done.2
  29.0 19.2 %while.12 = (s32[]{:T(128)}, f32[2,768,1024]{2,1,0:T(8,128)}, f32[2,2,256,256]{3,2,0,1:T(8,128)S(1)}, s32[]{:T(128)}, s32[8,2]{0,1:T(2,128)S(1)}, /*index=5*/f32...) while((s32[]{:T(128)}, f32[2,768,1024]{2,1,0:T(8,128)}, ...), condition=%wide.region_4.5_spmd, body=%wide.region_0.4_spmd.sunk | while | flops 1082195968 | bytes 27525448 | solution.py:109
  29.7 0.1 constant_dynamic-slice_fusion.3
  29.8 0.6 fusion.63
  34.1 1.3 dynamic-slice_bitcast_fusion.3
  35.5 0.2 fusion.64
  35.6 0.4 convolution_convert_fusion.3
  36.1 0.5 convolution_bitcast_fusion.2
  36.6 0.1 fusion.66
  36.7 1.0 fusion.67
  37.7 0.2 mul.321
  37.9 0.5 fusion.68
  38.4 0.5 fusion.70
  38.9 0.3 add_bitcast_fusion.2
  39.2 1.4 maximum_add_fusion.4
  40.6 0.3 maximum_add_fusion.5
  40.8 6.7 %dynamic_update_slice.4 = f32[2,768,1024]{2,1,0:T(8,128)} dynamic-update-slice(f32[2,768,1024]{2,1,0:T(8,128)} %get-tuple-element.198, f32[2,256,256]{2,1,0:T(8,128)S(1)} %maximum_add_fusion.4, s32[]{:T(128)} %constant.12.clone.1..sunk, s32[]{:T(128)S(6)} %select_n.47, s32[]{:T(128)S(6)} %select_n.48) | dynamic-update-slice | bytes 1048580 | tf_op jit(solution)/shard_map/while/body/dynamic_update_slice | solution.py:81
  48.2 3.2 %slice.61 = f32[2,256,1024]{2,1,0:T(8,128)} slice(f32[2,768,1024]{2,1,0:T(8,128)} %get-tuple-element.51), slice={[0:2], [512:768], [0:1024]} | slice | bytes 4194304 | tf_op jit(solution)/shard_map/slice | solution.py:112
  51.4 151.8 %collective-permute-start.1 = (f32[2,256,1024]{2,1,0:T(8,128)}, f32[2,256,1024]{2,1,0:T(8,128)}, u32[]{:S(2)}, u32[]{:S(2)}) collective-permute-start(f32[2,256,1024]{2,1,0:T(8,128)} %slice.61), channel_id=1, source_target_pairs={{0,1},{1,2},{2,3},{3,4},{4,5},{5,6},{6,7},{7,8},{8,9},{9,10},{10,1... | collective-permute-start | bytes 6291464 | tf_op jit(solution)/shard_map/ppermute | solution.py:12
  203.2 1.0 copy.11
  204.2 0.0 all-reduce.3.cloned.1.call-update
  204.2 94.0 %all-reduce.3.cloned.1.call-done = f32[1024,256]{1,0:T(8,128)} async-done(((f32[1024,256]{1,0:T(8,128)}), f32[1024,256]{1,0:T(8,128)}) %all-reduce.3.cloned.1.call-update) | async-done | bytes 1048592 | tf_op jit(solution)/shard_map/psum | solution.py:117
  298.2 1.5 constant_dynamic-slice_fusion.1
  299.7 0.0 collective-permute-done.1
  299.7 5.8 %pad_add_fusion = f32[2,512,1024]{2,1,0:T(8,128)} fusion(f32[2,256,1024]{2,1,0:T(8,128)} %collective-permute-done.1, f32[2,768,1024]{2,1,0:T(8,128)} %get-tuple-element.51), kind=kLoop, calls=%fused_computation.54 | loop fusion | flops 1048576 | bytes 10485760 | tf_op jit(solution)/shard_map/add | solution.py:113
  (4 shorter events, 0.1 us)
Async XLA Ops:
  7.2 4.6 %copy-start.1 = (f32[2,2,256,256]{3,2,1,0:T(8,128)S(1)}, f32[2,2,256,256]{3,2,1,0:T(8,128)}, u32[]{:S(2)}) copy-start(f32[2,2,256,256]{3,2,1,0:T(8,128)} %param.8) | copy-start | bytes 3145732
  7.2 291.0 %all-reduce.3.cloned.1.call-start = ((), (), s32[]{:S(2)}) async-start(), calls=%async_computation | async-start | bytes 2097152 | tf_op jit(solution)/shard_map/psum | solution.py:117
  10.5 9.9 %collective-permute-start = (f32[2,256,1024]{2,1,0:T(8,128)}, f32[2,256,1024]{2,1,0:T(8,128)}, u32[]{:S(2)}, u32[]{:S(2)}) collective-permute-start(f32[2,256,1024]{2,1,0:T(8,128)} %slice.59), channel_id=1, source_target_pairs={{1,0},{2,1},{3,2},{4,3},{5,4},{6,5},{7,6},{8,7},{9,8},{10,9},{11,1... | collective-permute-start | bytes 6291464 | tf_op jit(solution)/shard_map/ppermute | solution.py:12
  14.8 5.6 %copy-start = (f32[2,512,1024]{2,1,0:T(8,128)S(1)}, f32[2,512,1024]{2,1,0:T(8,128)}, u32[]{:S(2)}) copy-start(f32[2,512,1024]{2,1,0:T(8,128)} %param.7) | copy-start | bytes 12582916
  25.5 3.5 %copy-start.2 = (s32[1,8,2]{1,2,0:T(2,128)S(1)}, s32[1,8,2]{1,2,0:T(2,128)}, u32[]{:S(2)}) copy-start(s32[1,8,2]{1,2,0:T(2,128)} %param.9) | copy-start | bytes 196
  51.4 248.3 %collective-permute-start.1 = (f32[2,256,1024]{2,1,0:T(8,128)}, f32[2,256,1024]{2,1,0:T(8,128)}, u32[]{:S(2)}, u32[]{:S(2)}) collective-permute-start(f32[2,256,1024]{2,1,0:T(8,128)} %slice.61), channel_id=1, source_target_pairs={{0,1},{1,2},{2,3},{3,4},{4,5},{5,6},{6,7},{7,8},{8,9},{9,10},{10,1... | collective-permute-start | bytes 6291464 | tf_op jit(solution)/shard_map/ppermute | solution.py:12
Sparse Core Ops, SparseCore 0:
  204.4 93.8 all-reduce.2
where the time goes:
time: 315 us; the launch traced here: 312 us
  starting transfers between devices  153 us (49%)
  waiting for transfers between devices  94 us (30%)
  local copies, waits for them, and re-layouts  24.5 us (8%)
  other arithmetic  19.6 us (6%)
  between operations  14.1 us (4%)
  loops' own time  5.21 us (2%)
    ppermute x2, starting transfers between devices, shifted(): lax.ppermute(value, axis, [(source, source + steps) for source in range(i...  153 us
    psum x1, waiting for transfers between devices, on_device(): whole_probe = lax.psum(flat_probe, 'tr')  94 us
    dynamic_update_slice x1, local copies, waits for them, and re-layouts, add_block(): return lax.dynamic_update_slice(gradient, current + block, corner)  6.72 us
  transfers between devices with their start and end apart: 3, of which 1 were waited for; matrix products, arithmetic and copies ran while one was open for 4% of the time, Pallas kernels for 0%

commit v1 on v0

--- a/solution.py
+++ b/solution.py
@@ -114,7 +114,8 @@
         edge_grad, ((0, 0), (0, strip_rows - patch_size), (0, 0))
     )
     flat_probe = probe_sum.reshape(-1, patch_size)
-    whole_probe = lax.psum(flat_probe, "tr")
+    parts = lax.all_gather(flat_probe, "tr", axis=0, tiled=False)
+    whole_probe = parts.sum(axis=0)
     share_rows = flat_probe.shape[0] // lax.axis_size("tr")
     probe_grad = lax.dynamic_slice_in_dim(
         whole_probe, lax.axis_index("tr") * share_rows, share_rows, 0

time: 315 us -> 353 us (1.12)
  waiting for transfers between devices: 94 us -> 125 us
  other arithmetic: 19.6 us -> 26.4 us
    all_gather x0 -> x1, waiting for transfers between devices: none -> 121 us  [on_device(): parts = lax.all_gather(flat_probe, 'tr', axis=0, tiled=False)]
    psum x1 -> x0, waiting for transfers between devices: 94 us -> none  [on_device(): whole_probe = lax.psum(flat_probe, 'tr')]
    reduce_sum x0 -> x1, other arithmetic: none -> 6.98 us  [on_device(): whole_probe = parts.sum(axis=0)]
    ppermute x2, waiting for transfers between devices: 0.01 us -> 3.84 us  [shifted(): lax.ppermute(value, axis, [(source, source + steps) for source in range(i...]
  transfers between devices with their start and end apart: 3 -> 3, of which waited for: 1 -> 2; matrix products, arithmetic and copies ran while one was open for 4% -> 5% of each run, Pallas kernels for 0% -> 0%
where the time goes in v1:
time: 353 us; the launch traced here: 350 us
  starting transfers between devices  153 us (43%)
  waiting for transfers between devices  125 us (35%)
  other arithmetic  26.4 us (7%)
  local copies, waits for them, and re-layouts  23.7 us (7%)
  between operations  14.1 us (4%)
  loops' own time  5.42 us (2%)
    ppermute x2, starting transfers between devices, shifted(): lax.ppermute(value, axis, [(source, source + steps) for source in range(i...  153 us
    all_gather x1, waiting for transfers between devices, on_device(): parts = lax.all_gather(flat_probe, 'tr', axis=0, tiled=False)  121 us
  transfers between devices with their start and end apart: 3, of which 2 were waited for; matrix products, arithmetic and copies ran while one was open for 5% of the time, Pallas kernels for 0%

profile of v1, /device:TPU:0, one launch (start us, length us, event | category | flops | bytes accessed | tf_op | source)
XLA Modules:
  0.0 349.8 jit_solution(16201542866637692058)
XLA Ops:
  7.2 0.0 copy-start.1
  7.2 0.0 all-gather.2.cloned.1.call-start
  7.2 3.2 slice.59
  10.5 1.3 collective-permute-start
  11.7 0.0 copy-done.1
  11.8 0.1 copy.19
  11.8 2.9 copy.18
  14.8 0.0 copy-start
  14.8 1.0 fusion.37
  15.8 1.1 negate_convert_fusion
  16.9 3.5 sqrt_bitcast_fusion
  20.4 0.0 collective-permute-done
  20.4 0.0 copy-done
  20.4 5.1 %pad_maximum_fusion = f32[2,768,1024]{2,1,0:T(8,128)} fusion(f32[2,256,1024]{2,1,0:T(8,128)} %collective-permute-done, f32[2,512,1024]{2,1,0:T(8,128)S(1)} %copy-done), kind=kLoop, calls=%fused_computation.53 | loop fusion | flops 1572864 | bytes 12582912 | tf_op jit(solution)/shard_map/concatenate | solution.py:89
  25.5 0.0 copy-start.2
  25.5 0.1 broadcast_in_dim.10
  25.6 3.4 broadcast_in_dim.4
  29.0 0.0 copy-done.2
  29.0 19.4 %while.12 = (s32[]{:T(128)}, f32[2,768,1024]{2,1,0:T(8,128)}, f32[2,2,256,256]{3,2,0,1:T(8,128)S(1)}, s32[]{:T(128)}, s32[8,2]{0,1:T(2,128)S(1)}, /*index=5*/f32...) while((s32[]{:T(128)}, f32[2,768,1024]{2,1,0:T(8,128)}, ...), condition=%wide.region_4.5_spmd, body=%wide.region_0.4_spmd.sunk | while | flops 1082195968 | bytes 27525448 | solution.py:109
  29.7 0.1 constant_dynamic-slice_fusion.3
  29.8 0.6 fusion.63
  34.4 1.3 dynamic-slice_bitcast_fusion.3
  35.7 0.2 fusion.64
  35.9 0.4 convolution_convert_fusion.3
  36.4 0.5 convolution_bitcast_fusion.2
  36.8 0.1 fusion.66
  36.9 1.0 fusion.67
  37.9 0.2 mul.321
  38.2 0.5 fusion.68
  38.7 0.5 fusion.70
  39.2 0.3 add_bitcast_fusion.2
  39.5 1.4 maximum_add_fusion.4
  40.8 0.3 maximum_add_fusion.5
  41.1 6.7 %dynamic_update_slice.4 = f32[2,768,1024]{2,1,0:T(8,128)} dynamic-update-slice(f32[2,768,1024]{2,1,0:T(8,128)} %get-tuple-element.216, f32[2,256,256]{2,1,0:T(8,128)S(1)} %maximum_add_fusion.4, s32[]{:T(128)} %constant.13.clone.1..sunk, s32[]{:T(128)S(6)} %select_n.47, s32[]{:T(128)S(6)} %select_n.48) | dynamic-update-slice | bytes 1048580 | tf_op jit(solution)/shard_map/while/body/dynamic_update_slice | solution.py:81
  48.5 1.1 copy.20
  49.5 0.0 all-gather.2.cloned.1.call-update
  49.6 3.2 slice.61
  52.7 152.1 %collective-permute-start.1 = (f32[2,256,1024]{2,1,0:T(8,128)}, f32[2,256,1024]{2,1,0:T(8,128)S(1)}, u32[]{:S(2)}, u32[]{:S(2)}) collective-permute-start(f32[2,256,1024]{2,1,0:T(8,128)} %slice.61), channel_id=1, source_target_pairs={{0,1},{1,2},{2,3},{3,4},{4,5},{5,6},{6,7},{7,8},{8,9},{9,10},{10,1... | collective-permute-start | bytes 6291464 | tf_op jit(solution)/shard_map/ppermute | solution.py:12
  204.9 3.8 %collective-permute-done.1 = f32[2,256,1024]{2,1,0:T(8,128)S(1)} collective-permute-done((f32[2,256,1024]{2,1,0:T(8,128)}, f32[2,256,1024]{2,1,0:T(8,128)S(1)}, u32[]{:S(2)}, u32[]{:S(2)}) %collective-permute-start.1) | collective-permute-done | bytes 2097184 | tf_op jit(solution)/shard_map/ppermute | solution.py:12
  208.7 5.6 %pad_add_fusion = f32[2,512,1024]{2,1,0:T(8,128)} fusion(f32[2,256,1024]{2,1,0:T(8,128)S(1)} %collective-permute-done.1, f32[2,768,1024]{2,1,0:T(8,128)} %get-tuple-element.51), kind=kLoop, calls=%fused_computation.54 | loop fusion | flops 1048576 | bytes 10485760 | tf_op jit(solution)/shard_map/add | solution.py:113
  214.3 121.0 %all-gather.2.cloned.1.call-done = f32[16,1024,256]{2,1,0:T(8,128)} async-done(((f32[1,1024,256]{2,1,0:T(8,128)}), f32[16,1024,256]{2,1,0:T(8,128)}) %all-gather.2.cloned.1.call-update) | async-done | bytes 16777232 | tf_op jit(solution)/shard_map/all_gather | solution.py:117
  335.3 7.0 %reduce_sum.36 = f32[1024,256]{1,0:T(8,128)S(1)} reduce(f32[16,1024,256]{2,1,0:T(8,128)} %all-gather.2.cloned.1.call-done, f32[]{:T(128)} %constant.22.clone.1), dimensions={0}, to_apply=%region_5.6 | reduce | flops 3932160 | bytes 17825796 | tf_op jit(solution)/shard_map/reduce_sum | solution.py:118
  342.3 0.6 constant_dynamic-slice_fusion.1
  (4 shorter events, 0.1 us)
Async XLA Ops:
  7.2 4.6 %copy-start.1 = (f32[2,2,256,256]{3,2,1,0:T(8,128)S(1)}, f32[2,2,256,256]{3,2,1,0:T(8,128)}, u32[]{:S(2)}) copy-start(f32[2,2,256,256]{3,2,1,0:T(8,128)} %param.8) | copy-start | bytes 3145732
  7.2 328.1 %all-gather.2.cloned.1.call-start = ((), (), s32[]{:S(2)}) async-start(), calls=%async_computation | async-start | bytes 17825792 | tf_op jit(solution)/shard_map/all_gather | solution.py:117
  10.5 9.9 %collective-permute-start = (f32[2,256,1024]{2,1,0:T(8,128)}, f32[2,256,1024]{2,1,0:T(8,128)}, u32[]{:S(2)}, u32[]{:S(2)}) collective-permute-start(f32[2,256,1024]{2,1,0:T(8,128)} %slice.59), channel_id=1, source_target_pairs={{1,0},{2,1},{3,2},{4,3},{5,4},{6,5},{7,6},{8,7},{9,8},{10,9},{11,1... | collective-permute-start | bytes 6291464 | tf_op jit(solution)/shard_map/ppermute | solution.py:12
  14.8 5.6 %copy-start = (f32[2,512,1024]{2,1,0:T(8,128)S(1)}, f32[2,512,1024]{2,1,0:T(8,128)}, u32[]{:S(2)}) copy-start(f32[2,512,1024]{2,1,0:T(8,128)} %param.7) | copy-start | bytes 12582916
  25.5 3.5 %copy-start.2 = (s32[1,8,2]{1,2,0:T(2,128)S(1)}, s32[1,8,2]{1,2,0:T(2,128)}, u32[]{:S(2)}) copy-start(s32[1,8,2]{1,2,0:T(2,128)} %param.9) | copy-start | bytes 196
  52.7 156.0 %collective-permute-start.1 = (f32[2,256,1024]{2,1,0:T(8,128)}, f32[2,256,1024]{2,1,0:T(8,128)S(1)}, u32[]{:S(2)}, u32[]{:S(2)}) collective-permute-start(f32[2,256,1024]{2,1,0:T(8,128)} %slice.61), channel_id=1, source_target_pairs={{0,1},{1,2},{2,3},{3,4},{4,5},{5,6},{6,7},{7,8},{8,9},{9,10},{10,1... | collective-permute-start | bytes 6291464 | tf_op jit(solution)/shard_map/ppermute | solution.py:12
Sparse Core Ops, SparseCore 0:
  49.7 285.5 all-gather.1
